TPU v7x, 32 devices: a whole 2x2x4 slice. The times are simulated.
32 devices in a mesh: batch: 4 (over x, core), neuron: 8 (over z, y).
Axes of the slice: x: 2, y: 2, z: 4, core: 2. Of those that a mesh axis runs over, the one named last changes fastest.
Arguments:
- tokens: bfloat16 [2, 256, 12288], P(None, 'neuron', 'batch'), may hold values from -6 to 6
- ln_gain: float32 [12288], P('batch'), may hold values from 0.25 to 1.75
- ln_bias: float32 [12288], P('batch'), may hold values from -3 to 3
- up_weight: bfloat16 [12288, 24576], P('batch', 'neuron'), may hold values from -0.0546875 to 0.0546875
- up_bias: float32 [24576], P('neuron'), may hold values from -3 to 3
- down_weight: bfloat16 [24576, 12288], P('neuron', 'batch'), may hold values from -0.078125 to 0.078125
- down_bias: float32 [12288], P('batch'), may hold values from -3 to 3
- active: int32 [2, 2, 48], replicated, may hold values from 0 to 191, all different within a row
Outputs:
- mixed: bfloat16 [2, 256, 12288], P(None, 'neuron', 'batch')
Inputs may be any that keep to these rules, and one draw needn't show every extreme that they name: `active`: each row block of each; despite its name it splits features, not a batch step lists 48 distinct neuron block numbers; every number appears in some list.
All inputs are finite; a program needn't handle non-finite values.
Results may differ from a plain program's by a relative error of at most 0.0044.
Values may be sent and summed in bfloat16 or wider, within the bound.
No kernel may reach another device: no remote copies, remote signals or barrier semaphores. Data moves between devices by JAX's collectives and lax.ppermute only.
A program may use at most 128 MiB of HBM per device.

v0:
```python
import jax
import jax.numpy as jnp
from jax import lax
from jax.sharding import PartitionSpec as P

D = 12288
BLK = 128
RB = 128
STEPS = 2
epsilon = 1e-05


def local_table(listed, first_block, local_blocks):
    block_ids = first_block + jnp.arange(local_blocks, dtype=jnp.int32)
    return jnp.any(listed[:, :, None] == block_ids[None, None, :], axis=1).astype(jnp.float32)


def activate(preact, up_bias, table, first_row):
    row_total = preact.shape[0]
    local_blocks = table.shape[1]
    row_blocks = (first_row + jnp.arange(row_total, dtype=jnp.int32)) // RB
    block_count = table.shape[0]
    onehot = (row_blocks[:, None] == jnp.arange(block_count, dtype=jnp.int32)[None, :]).astype(
        jnp.float32
    )
    row_mask = jnp.dot(onehot, table, preferred_element_type=jnp.float32)
    shaped = jnp.maximum(preact + up_bias, 0.0).reshape(row_total, local_blocks, BLK)
    return (
        (shaped * row_mask[:, :, None]).reshape(row_total, local_blocks * BLK).astype(jnp.bfloat16)
    )


def normalize(inputs, sum_total, square_total, ln_gain, ln_bias):
    average = sum_total / D
    spread = square_total / D - average * average
    scaled = (inputs - average[:, None]) * lax.rsqrt(spread + epsilon)[:, None]
    return (scaled * ln_gain + ln_bias).astype(jnp.bfloat16)


def local(tokens, ln_gain, ln_bias, up_weight, up_bias, down_weight, down_bias, active):
    local_rows = tokens.shape[1]
    local_neurons = up_weight.shape[1]
    local_blocks = local_neurons // BLK
    neuron_index = lax.axis_index("neuron")
    batch_index = lax.axis_index("batch")
    all_rows = local_rows * lax.axis_size("neuron")
    share_rows = all_rows // lax.axis_size("batch")
    first_block = neuron_index * local_blocks
    results = []
    for step_index in range(STEPS):
        residual = tokens[step_index]
        residual_wide = residual.astype(jnp.float32)
        table = local_table(active[step_index], first_block, local_blocks)
        sum_total, square_total = lax.psum(
            (jnp.sum(residual_wide, axis=-1), jnp.sum(residual_wide * residual_wide, axis=-1)),
            "batch",
        )
        normed = normalize(residual_wide, sum_total, square_total, ln_gain, ln_bias)
        gathered = lax.all_gather(normed, "neuron", axis=0, tiled=True)
        preact = lax.psum_scatter(
            jnp.dot(gathered, up_weight, preferred_element_type=jnp.float32),
            "batch",
            scatter_dimension=0,
            tiled=True,
        )
        hidden_share = activate(preact, up_bias, table, batch_index * share_rows)
        hidden_all = lax.all_gather(hidden_share, "batch", axis=0, tiled=True)
        projected = lax.psum_scatter(
            jnp.dot(hidden_all, down_weight, preferred_element_type=jnp.float32),
            "neuron",
            scatter_dimension=0,
            tiled=True,
        )
        results.append((projected + residual_wide + down_bias).astype(jnp.bfloat16))
    return jnp.stack(results)


def solution(mesh):
    in_specs = (
        P(None, "neuron", "batch"),
        P("batch"),
        P("batch"),
        P("batch", "neuron"),
        P("neuron"),
        P("neuron", "batch"),
        P("batch"),
        P(),
    )
    out_specs = P(None, "neuron", "batch")
    return jax.shard_map(local, mesh=mesh, in_specs=in_specs, out_specs=out_specs, check_vma=False)
```

profile of v0, /device:TPU:0, one launch (start us, length us, event | category | flops | bytes accessed | tf_op | source)
XLA Modules:
  0.0 396.0 jit_solution(5214317015410200735)
XLA Ops:
  6.5 1.2 convert_reduce_fusion.1
  7.7 1.2 fusion.12
  8.9 8.4 %all-reduce = (f32[32]{0:T(128)S(1)}, f32[32]{0:T(128)S(1)}, f32[32]{0:T(128)S(1)}, f32[32]{0:T(128)S(1)}) all-reduce(f32[32]{0:T(128)S(1)} %get-tuple-element.8, f32[32]{0:T(128)S(1)} %get-tuple-element.6, f32[32]{0:T(128)S(1)} %get-tuple-element.7, f32[32]{0:T(128)S(1)} %get-tuple-element.5), channel_id=1, replica_groups=mesh['batch'=4,'neuron'=8] {'batch'}, use_global_device_ids=true, to_apply=%region_10.11 | all-reduce | flops 128 | bytes 1024 | tf_op jit(solution)/shard_map/psum | solution.py:54
  17.3 2.0 fusion.11
  19.4 0.7 all-gather.9.cloned.1.call-update
  20.1 43.9 %all-gather.5.cloned.1.call-done = bf16[256,3072]{1,0:T(8,128)(2,1)} async-done(((bf16[32,3072]{1,0:T(8,128)(2,1)}), bf16[256,3072]{1,0:T(8,128)(2,1)}) %all-gather.5.cloned.1.call-update) | async-done | bytes 1572880 | tf_op jit(solution)/shard_map/all_gather | solution.py:59
  64.0 10.6 %fusion.28 = f32[256,3072]{1,0:T(8,128)} fusion(bf16[256,3072]{1,0:T(8,128)(2,1)} %all-gather.5.cloned.1.call-done, bf16[3072,3072]{1,0:T(8,128)(2,1)} %param.11), kind=kOutput, calls=%fused_computation.49 | convolution fusion | flops 4831838208 | bytes 23592960 | tf_op jit(solution)/shard_map/dot_general | solution.py:61
  74.6 34.2 %all-gather.9.cloned.1.call-done = bf16[256,3072]{1,0:T(8,128)(2,1)} async-done(((bf16[32,3072]{1,0:T(8,128)(2,1)}), bf16[256,3072]{1,0:T(8,128)(2,1)}) %all-gather.9.cloned.1.call-update) | async-done | bytes 1572880 | tf_op jit(solution)/shard_map/all_gather | solution.py:59
  108.8 11.1 %fusion.30 = f32[256,3072]{1,0:T(8,128)} fusion(bf16[256,3072]{1,0:T(8,128)(2,1)} %all-gather.9.cloned.1.call-done, bf16[3072,3072]{1,0:T(8,128)(2,1)} %param.11), kind=kOutput, calls=%fused_computation.51 | convolution fusion | flops 4831838208 | bytes 23592960 | tf_op jit(solution)/shard_map/dot_general | solution.py:61
  120.0 0.6 copy-done.3
  121.2 26.4 %reduce-scatter.5.cloned.1.call-done = f32[64,3072]{1,0:T(8,128)} async-done(((f32[256,3072]{1,0:T(8,128)}), f32[64,3072]{1,0:T(8,128)}) %reduce-scatter.5.cloned.1.call-update) | async-done | bytes 786448 | tf_op jit(solution)/shard_map/reduce_scatter | solution.py:60
  147.6 40.3 %reduce-scatter.9.cloned.1.call-done = f32[64,3072]{1,0:T(8,128)} async-done(((f32[256,3072]{1,0:T(8,128)}), f32[64,3072]{1,0:T(8,128)}) %reduce-scatter.9.cloned.1.call-update) | async-done | bytes 786448 | tf_op jit(solution)/shard_map/reduce_scatter | solution.py:60
  187.9 0.3 mul.87
  188.2 0.3 mul.79
  188.5 2.7 fusion.1
  191.2 0.5 all-gather.7.cloned.1.call-update
  191.8 19.2 %all-gather.11.cloned.1.call-done = bf16[256,3072]{1,0:T(8,128)(2,1)} async-done(((bf16[64,3072]{1,0:T(8,128)(2,1)}), bf16[256,3072]{1,0:T(8,128)(2,1)}) %all-gather.11.cloned.1.call-update) | async-done | bytes 1572880 | tf_op jit(solution)/shard_map/all_gather | solution.py:67
  211.0 10.6 %fusion.31 = f32[256,3072]{1,0:T(8,128)} fusion(bf16[256,3072]{1,0:T(8,128)(2,1)} %all-gather.11.cloned.1.call-done, bf16[3072,3072]{1,0:T(8,128)(2,1)} %param.13), kind=kOutput, calls=%fused_computation.52 | convolution fusion | flops 4831838208 | bytes 23592960 | tf_op jit(solution)/shard_map/dot_general | solution.py:69
  221.6 10.4 %all-gather.7.cloned.1.call-done = bf16[256,3072]{1,0:T(8,128)(2,1)} async-done(((bf16[64,3072]{1,0:T(8,128)(2,1)}), bf16[256,3072]{1,0:T(8,128)(2,1)}) %all-gather.7.cloned.1.call-update) | async-done | bytes 1572880 | tf_op jit(solution)/shard_map/all_gather | solution.py:67
  232.1 10.6 %fusion.29 = f32[256,3072]{1,0:T(8,128)} fusion(bf16[256,3072]{1,0:T(8,128)(2,1)} %all-gather.7.cloned.1.call-done, bf16[3072,3072]{1,0:T(8,128)(2,1)} %param.13), kind=kOutput, calls=%fused_computation.50 | convolution fusion | flops 4831838208 | bytes 23592960 | tf_op jit(solution)/shard_map/dot_general | solution.py:69
  242.7 67.5 %reduce-scatter.11.cloned.1.call-done = f32[32,3072]{1,0:T(8,128)} async-done(((f32[256,3072]{1,0:T(8,128)}), f32[32,3072]{1,0:T(8,128)}) %reduce-scatter.11.cloned.1.call-update) | async-done | bytes 393232 | tf_op jit(solution)/shard_map/reduce_scatter | solution.py:68
  310.1 77.1 %reduce-scatter.7.cloned.1.call-done = f32[32,3072]{1,0:T(8,128)} async-done(((f32[256,3072]{1,0:T(8,128)}), f32[32,3072]{1,0:T(8,128)}) %reduce-scatter.7.cloned.1.call-update) | async-done | bytes 393232 | tf_op jit(solution)/shard_map/reduce_scatter | solution.py:68
  387.2 1.2 fusion.23
  388.4 0.7 copy-done.4
  (30 shorter events, 1.0 us)
Async XLA Ops:
  6.5 57.5 %all-gather.5.cloned.1.call-start = ((), (), s32[]{:S(2)}) async-start(), calls=%async_computation.4 | async-start | bytes 1769472 | tf_op jit(solution)/shard_map/all_gather | solution.py:59
  19.3 89.5 %all-gather.9.cloned.1.call-start = ((), (), s32[]{:S(2)}) async-start(), calls=%async_computation.8 | async-start | bytes 1769472 | tf_op jit(solution)/shard_map/all_gather | solution.py:59
  20.1 127.5 %reduce-scatter.5.cloned.1.call-start = ((), (), s32[]{:S(2)}) async-start(), calls=%async_computation.5 | async-start | bytes 3932160 | tf_op jit(solution)/shard_map/reduce_scatter | solution.py:60
  74.6 113.3 %reduce-scatter.9.cloned.1.call-start = ((), (), s32[]{:S(2)}) async-start(), calls=%async_computation.9 | async-start | bytes 3932160 | tf_op jit(solution)/shard_map/reduce_scatter | solution.py:60
  119.9 0.7 copy-start.3
  119.9 68.6 %copy-start.1 = (f32[3072]{0:T(1024)S(1)}, f32[3072]{0:T(1024)}, u32[]{:S(2)}) copy-start(f32[3072]{0:T(1024)} %param.12) | copy-start | bytes 36868
  119.9 91.1 %all-gather.11.cloned.1.call-start = ((), (), s32[]{:S(2)}) async-start(), calls=%async_computation.10 | async-start | bytes 1966080 | tf_op jit(solution)/shard_map/all_gather | solution.py:67
  191.2 40.9 %all-gather.7.cloned.1.call-start = ((), (), s32[]{:S(2)}) async-start(), calls=%async_computation.6 | async-start | bytes 1966080 | tf_op jit(solution)/shard_map/all_gather | solution.py:67
  191.8 118.4 %reduce-scatter.11.cloned.1.call-start = ((), (), s32[]{:S(2)}) async-start(), calls=%async_computation.11 | async-start | bytes 3538944 | tf_op jit(solution)/shard_map/reduce_scatter | solution.py:68
  221.6 165.6 %reduce-scatter.7.cloned.1.call-start = ((), (), s32[]{:S(2)}) async-start(), calls=%async_computation.7 | async-start | bytes 3538944 | tf_op jit(solution)/shard_map/reduce_scatter | solution.py:68
  242.6 144.6 %copy-start = (bf16[2,32,3072]{2,1,0:T(8,128)(2,1)S(1)}, bf16[2,32,3072]{2,1,0:T(8,128)(2,1)}, u32[]{:S(2)}) copy-start(bf16[2,32,3072]{2,1,0:T(8,128)(2,1)} %param.8) | copy-start | bytes 1179652
  242.6 144.6 %copy-start.2 = (f32[3072]{0:T(1024)S(1)}, f32[3072]{0:T(1024)}, u32[]{:S(2)}) copy-start(f32[3072]{0:T(1024)} %param.14) | copy-start | bytes 36868
  388.4 0.7 copy-start.4
Sparse Core Ops, SparseCore 0:
  19.5 44.4 all-gather.4
  66.2 42.5 all-gather.8
  111.4 36.2 reduce-scatter.4
  150.0 37.8 reduce-scatter.8
  191.3 19.6 all-gather.10
  212.4 19.6 all-gather.6
  235.6 74.4 reduce-scatter.10
  313.7 73.4 reduce-scatter.6
where the time goes:
time: 396 us
  waiting for transfers between devices  320 us (81%)
  matrix products  43.2 us (11%)
  between operations  13.6 us (3%)
  other arithmetic  8.54 us (2%)
  blocking collectives  8.37 us (2%)
    reduce_scatter x2, waiting for transfers between devices, local(): lax.psum_scatter(jnp.dot(hidden_all, down_weight, preferred_element_type=...  145 us
    all_gather x2, waiting for transfers between devices, local(): gathered = lax.all_gather(normed, 'neuron', axis=0, tiled=True)  78 us
    reduce_scatter x2, waiting for transfers between devices, local(): lax.psum_scatter(jnp.dot(gathered, up_weight, preferred_element_type=jnp....  66.7 us
    all_gather x2, waiting for transfers between devices, local(): hidden_all = lax.all_gather(hidden_share, 'batch', axis=0, tiled=True)  29.6 us
    dot_general x2, matrix products, local(): jnp.dot(gathered, up_weight, preferred_element_type=jnp.float32)  21.6 us
    dot_general x2, matrix products, local(): jnp.dot(hidden_all, down_weight, preferred_element_type=jnp.float32)  21.2 us
    psum x1, blocking collectives, local(): lax.psum((jnp.sum(residual_wide, axis=-1), jnp.sum(residual_wide * residu...  8.37 us
  transfers between devices with their start and end apart: 8, of which 8 were waited for; matrix products, arithmetic and copies ran while one was open for 11% of the time, Pallas kernels for 0%

commit v1 on v0

--- a/solution.py
+++ b/solution.py
@@ -1,3 +1,4 @@
+import functools
 import jax
 import jax.numpy as jnp
 from jax import lax
@@ -8,6 +9,24 @@
 RB = 128
 STEPS = 2
 epsilon = 1e-05
+
+
+def _deliver_counts(matrix, along_axis):
+    view_out = lax.axis_size(along_axis)
+    v_next, y1 = (view_out, lax.axis_index(along_axis))
+    clean, plain = (matrix, 1)
+    while plain < v_next:
+        oldest = lax.ppermute(
+            clean, axis_name=along_axis, perm=[(dev_i, dev_i ^ plain) for dev_i in range(v_next)]
+        )
+        now = jnp.concatenate([clean, oldest], axis=0)
+        far_arr = jnp.concatenate([oldest, clean], axis=0)
+        clean = jnp.where(y1 & plain == 0, now, far_arr)
+        plain = 2 * plain
+    return clean
+
+
+marks_map = functools.partial(_deliver_counts, along_axis="neuron")
 
 
 def local_table(listed, first_block, local_blocks):
@@ -56,7 +75,7 @@
             "batch",
         )
         normed = normalize(residual_wide, sum_total, square_total, ln_gain, ln_bias)
-        gathered = lax.all_gather(normed, "neuron", axis=0, tiled=True)
+        gathered = marks_map(normed)
         preact = lax.psum_scatter(
             jnp.dot(gathered, up_weight, preferred_element_type=jnp.float32),
             "batch",

time: 396 us -> 390 us (0.985)
  waiting for transfers between devices: 320 us -> 302 us
  starting transfers between devices: 0.29 us -> 13.9 us
    ppermute x0 -> x6, waiting for transfers between devices: none -> 87.2 us  [_deliver_counts(): lax.ppermute(clean, axis_name=along_axis, perm=[(dev_i, dev_i ^ plain) fo...]
    all_gather x2 -> x0, waiting for transfers between devices: 78 us -> none  [local(): gathered = lax.all_gather(normed, 'neuron', axis=0, tiled=True)]
    reduce_scatter x2, waiting for transfers between devices: 66.7 us -> 40.4 us  [local(): lax.psum_scatter(jnp.dot(gathered, up_weight, preferred_element_type=jnp....]
    ppermute x0 -> x6, starting transfers between devices: none -> 13.7 us  [_deliver_counts(): lax.ppermute(clean, axis_name=along_axis, perm=[(dev_i, dev_i ^ plain) fo...]
  transfers between devices with their start and end apart: 8 -> 12, of which waited for: 8 -> 11; matrix products, arithmetic and copies ran while one was open for 11% -> 8% of each run, Pallas kernels for 0% -> 0%
where the time goes in v1:
time: 390 us
  waiting for transfers between devices  302 us (77%)
  matrix products  43 us (11%)
  starting transfers between devices  13.9 us (4%)
  between operations  13.6 us (3%)
  blocking collectives  8.37 us (2%)
  other arithmetic  6.87 us (2%)
    reduce_scatter x2, waiting for transfers between devices, local(): lax.psum_scatter(jnp.dot(hidden_all, down_weight, preferred_element_type=...  144 us
    ppermute x6, waiting for transfers between devices, _deliver_counts(): lax.ppermute(clean, axis_name=along_axis, perm=[(dev_i, dev_i ^ plain) fo...  87.2 us
    reduce_scatter x2, waiting for transfers between devices, local(): lax.psum_scatter(jnp.dot(gathered, up_weight, preferred_element_type=jnp....  40.4 us
    all_gather x2, waiting for transfers between devices, local(): hidden_all = lax.all_gather(hidden_share, 'batch', axis=0, tiled=True)  29.6 us
    dot_general x2, matrix products, local(): jnp.dot(gathered, up_weight, preferred_element_type=jnp.float32)  21.5 us
    dot_general x2, matrix products, local(): jnp.dot(hidden_all, down_weight, preferred_element_type=jnp.float32)  21.1 us
    ppermute x6, starting transfers between devices, _deliver_counts(): lax.ppermute(clean, axis_name=along_axis, perm=[(dev_i, dev_i ^ plain) fo...  13.7 us
    psum x1, blocking collectives, local(): lax.psum((jnp.sum(residual_wide, axis=-1), jnp.sum(residual_wide * residu...  8.37 us
  transfers between devices with their start and end apart: 12, of which 11 were waited for; matrix products, arithmetic and copies ran while one was open for 8% of the time, Pallas kernels for 0%

profile of v1, /device:TPU:0, one launch (start us, length us, event | category | flops | bytes accessed | tf_op | source)
XLA Modules:
  0.0 390.1 jit_solution(10243832995422185104)
XLA Ops:
  8.9 8.4 %all-reduce = (f32[32]{0:T(128)S(1)}, f32[32]{0:T(128)S(1)}, f32[32]{0:T(128)S(1)}, f32[32]{0:T(128)S(1)}) all-reduce(f32[32]{0:T(128)S(1)} %get-tuple-element.8, f32[32]{0:T(128)S(1)} %get-tuple-element.6, f32[32]{0:T(128)S(1)} %get-tuple-element.7, f32[32]{0:T(128)S(1)} %get-tuple-element.5), channel_id=1, replica_groups=mesh['batch'=4,'neuron'=8] {'batch'}, use_global_device_ids=true, to_apply=%region_10.11 | all-reduce | flops 128 | bytes 1024 | tf_op jit(solution)/shard_map/psum | solution.py:73
  17.3 1.3 fusion.25
  18.6 1.6 collective-permute-start.3
  20.2 4.2 %collective-permute-done.3 = bf16[32,3072]{1,0:T(8,128)(2,1)S(1)} collective-permute-done((bf16[32,3072]{1,0:T(8,128)(2,1)S(1)}, bf16[32,3072]{1,0:T(8,128)(2,1)S(1)}, u32[]{:S(2)}, u32[]{:S(2)}) %collective-permute-start.3) | collective-permute-done | bytes 196640 | tf_op jit(solution)/shard_map/ppermute | solution.py:19
  24.4 1.6 collective-permute-start.4
  26.0 6.8 %collective-permute-done.4 = bf16[64,3072]{1,0:T(8,128)(2,1)S(1)} collective-permute-done((bf16[64,3072]{1,0:T(8,128)(2,1)S(1)}, bf16[64,3072]{1,0:T(8,128)(2,1)S(1)}, u32[]{:S(2)}, u32[]{:S(2)}) %collective-permute-start.4) | collective-permute-done | bytes 393248 | tf_op jit(solution)/shard_map/ppermute | solution.py:19
  33.0 3.5 collective-permute-start.5
  36.4 30.5 %collective-permute-done.5 = bf16[128,3072]{1,0:T(8,128)(2,1)S(1)} collective-permute-done((bf16[128,3072]{1,0:T(8,128)(2,1)S(1)}, bf16[128,3072]{1,0:T(8,128)(2,1)S(1)}, u32[]{:S(2)}, u32[]{:S(2)}) %collective-permute-start.5) | collective-permute-done | bytes 786464 | tf_op jit(solution)/shard_map/ppermute | solution.py:19
  67.0 10.7 %fusion.6 = f32[256,3072]{1,0:T(8,128)} fusion(bf16[3072,3072]{1,0:T(8,128)(2,1)} %param.11, bf16[128,3072]{1,0:T(8,128)(2,1)S(1)} %collective-permute-done.5, bf16[128,3072]{1,0:T(8,128)(2,1)S(1)} %maximum_select_fusion.5, pred[]{:T(512)S(6)} %eq.26), kind=kOutput, calls=%fused_computation.8 | convolution fusion | flops 4838916096 | bytes 23592960 | tf_op jit(solution)/shard_map/dot_general | solution.py:80
  77.7 1.6 collective-permute-start
  79.4 4.1 %collective-permute-done = bf16[32,3072]{1,0:T(8,128)(2,1)S(1)} collective-permute-done((bf16[32,3072]{1,0:T(8,128)(2,1)S(1)}, bf16[32,3072]{1,0:T(8,128)(2,1)S(1)}, u32[]{:S(2)}, u32[]{:S(2)}) %collective-permute-start) | collective-permute-done | bytes 196640 | tf_op jit(solution)/shard_map/ppermute | solution.py:19
  83.5 1.9 collective-permute-start.1
  85.5 8.4 %collective-permute-done.1 = bf16[64,3072]{1,0:T(8,128)(2,1)S(1)} collective-permute-done((bf16[64,3072]{1,0:T(8,128)(2,1)S(1)}, bf16[64,3072]{1,0:T(8,128)(2,1)S(1)}, u32[]{:S(2)}, u32[]{:S(2)}) %collective-permute-start.1) | collective-permute-done | bytes 393248 | tf_op jit(solution)/shard_map/ppermute | solution.py:19
  94.1 3.5 collective-permute-start.2
  97.6 33.2 %collective-permute-done.2 = bf16[128,3072]{1,0:T(8,128)(2,1)S(1)} collective-permute-done((bf16[128,3072]{1,0:T(8,128)(2,1)S(1)}, bf16[128,3072]{1,0:T(8,128)(2,1)S(1)}, u32[]{:S(2)}, u32[]{:S(2)}) %collective-permute-start.2) | collective-permute-done | bytes 786464 | tf_op jit(solution)/shard_map/ppermute | solution.py:19
  130.7 10.8 %fusion = f32[256,3072]{1,0:T(8,128)} fusion(bf16[3072,3072]{1,0:T(8,128)(2,1)} %param.11, bf16[128,3072]{1,0:T(8,128)(2,1)S(1)} %collective-permute-done.2, bf16[128,3072]{1,0:T(8,128)(2,1)S(1)} %maximum_select_fusion.4, pred[]{:T(512)S(6)} %eq.26), kind=kOutput, calls=%fused_computation.1 | convolution fusion | flops 4838916096 | bytes 23592960 | tf_op jit(solution)/shard_map/dot_general | solution.py:80
  142.8 40.4 %reduce-scatter.5.cloned.1.call-done = f32[64,3072]{1,0:T(8,128)} async-done(((f32[256,3072]{1,0:T(8,128)}), f32[64,3072]{1,0:T(8,128)}) %reduce-scatter.5.cloned.1.call-update) | async-done | bytes 786448 | tf_op jit(solution)/shard_map/reduce_scatter | solution.py:79
  184.3 1.3 fusion.15
  186.3 19.2 %all-gather.5.cloned.1.call-done = bf16[256,3072]{1,0:T(8,128)(2,1)} async-done(((bf16[64,3072]{1,0:T(8,128)(2,1)}), bf16[256,3072]{1,0:T(8,128)(2,1)}) %all-gather.5.cloned.1.call-update) | async-done | bytes 1572880 | tf_op jit(solution)/shard_map/all_gather | solution.py:86
  205.4 10.5 %fusion.45 = f32[256,3072]{1,0:T(8,128)} fusion(bf16[256,3072]{1,0:T(8,128)(2,1)} %all-gather.5.cloned.1.call-done, bf16[3072,3072]{1,0:T(8,128)(2,1)} %param.13), kind=kOutput, calls=%fused_computation.72 | convolution fusion | flops 4831838208 | bytes 23592960 | tf_op jit(solution)/shard_map/dot_general | solution.py:88
  216.1 10.5 %all-gather.3.cloned.1.call-done = bf16[256,3072]{1,0:T(8,128)(2,1)} async-done(((bf16[64,3072]{1,0:T(8,128)(2,1)}), bf16[256,3072]{1,0:T(8,128)(2,1)}) %all-gather.3.cloned.1.call-update) | async-done | bytes 1572880 | tf_op jit(solution)/shard_map/all_gather | solution.py:86
  226.5 10.6 %fusion.44 = f32[256,3072]{1,0:T(8,128)} fusion(bf16[256,3072]{1,0:T(8,128)(2,1)} %all-gather.3.cloned.1.call-done, bf16[3072,3072]{1,0:T(8,128)(2,1)} %param.13), kind=kOutput, calls=%fused_computation.71 | convolution fusion | flops 4831838208 | bytes 23592960 | tf_op jit(solution)/shard_map/dot_general | solution.py:88
  237.2 67.0 %reduce-scatter.11.cloned.1.call-done = f32[32,3072]{1,0:T(8,128)} async-done(((f32[256,3072]{1,0:T(8,128)}), f32[32,3072]{1,0:T(8,128)}) %reduce-scatter.11.cloned.1.call-update) | async-done | bytes 393232 | tf_op jit(solution)/shard_map/reduce_scatter | solution.py:87
  304.1 77.2 %reduce-scatter.7.cloned.1.call-done = f32[32,3072]{1,0:T(8,128)} async-done(((f32[256,3072]{1,0:T(8,128)}), f32[32,3072]{1,0:T(8,128)}) %reduce-scatter.7.cloned.1.call-update) | async-done | bytes 393232 | tf_op jit(solution)/shard_map/reduce_scatter | solution.py:87
  (44 shorter events, 7.9 us)
Async XLA Ops:
  6.5 136.2 %reduce-scatter.9.cloned.1.call-start = ((), (), s32[]{:S(2)}) async-start(), calls=%async_computation.7 | async-start | bytes 3932160 | tf_op jit(solution)/shard_map/reduce_scatter | solution.py:79
  18.6 5.7 %collective-permute-start.3 = (bf16[32,3072]{1,0:T(8,128)(2,1)S(1)}, bf16[32,3072]{1,0:T(8,128)(2,1)S(1)}, u32[]{:S(2)}, u32[]{:S(2)}) collective-permute-start(bf16[32,3072]{1,0:T(8,128)(2,1)S(1)} %get-tuple-element.16), channel_id=1, source_target_pairs={{0,1},{1,0},{2,3},{3,2},{4,5},{5,4},{6,7},{7,6},{8,9},{9,8},{10,11... | collective-permute-start | bytes 589832 | tf_op jit(solution)/shard_map/ppermute | solution.py:19
  24.4 8.4 %collective-permute-start.4 = (bf16[64,3072]{1,0:T(8,128)(2,1)S(1)}, bf16[64,3072]{1,0:T(8,128)(2,1)S(1)}, u32[]{:S(2)}, u32[]{:S(2)}) collective-permute-start(bf16[64,3072]{1,0:T(8,128)(2,1)S(1)} %maximum_select_fusion.7), channel_id=1, source_target_pairs={{0,2},{1,3},{2,0},{3,1},{4,6},{5,7},{6,4},{7,5},{8,10},{9,11},{10,... | collective-permute-start | bytes 1179656 | tf_op jit(solution)/shard_map/ppermute | solution.py:19
  33.0 34.0 %collective-permute-start.5 = (bf16[128,3072]{1,0:T(8,128)(2,1)S(1)}, bf16[128,3072]{1,0:T(8,128)(2,1)S(1)}, u32[]{:S(2)}, u32[]{:S(2)}) collective-permute-start(bf16[128,3072]{1,0:T(8,128)(2,1)S(1)} %maximum_select_fusion.5), channel_id=1, source_target_pairs={{0,4},{1,5},{2,6},{3,7},{4,0},{5,1},{6,2},{7,3},{8,12},{9,13},{10,... | collective-permute-start | bytes 2359304 | tf_op jit(solution)/shard_map/ppermute | solution.py:19
  77.7 105.5 %reduce-scatter.5.cloned.1.call-start = ((), (), s32[]{:S(2)}) async-start(), calls=%async_computation.4 | async-start | bytes 3932160 | tf_op jit(solution)/shard_map/reduce_scatter | solution.py:79
  77.7 5.7 %collective-permute-start = (bf16[32,3072]{1,0:T(8,128)(2,1)S(1)}, bf16[32,3072]{1,0:T(8,128)(2,1)S(1)}, u32[]{:S(2)}, u32[]{:S(2)}) collective-permute-start(bf16[32,3072]{1,0:T(8,128)(2,1)S(1)} %get-tuple-element.15), channel_id=1, source_target_pairs={{0,1},{1,0},{2,3},{3,2},{4,5},{5,4},{6,7},{7,6},{8,9},{9,8},{10,11... | collective-permute-start | bytes 589832 | tf_op jit(solution)/shard_map/ppermute | solution.py:19
  83.5 10.4 %collective-permute-start.1 = (bf16[64,3072]{1,0:T(8,128)(2,1)S(1)}, bf16[64,3072]{1,0:T(8,128)(2,1)S(1)}, u32[]{:S(2)}, u32[]{:S(2)}) collective-permute-start(bf16[64,3072]{1,0:T(8,128)(2,1)S(1)} %maximum_select_fusion.6), channel_id=1, source_target_pairs={{0,2},{1,3},{2,0},{3,1},{4,6},{5,7},{6,4},{7,5},{8,10},{9,11},{10,... | collective-permute-start | bytes 1179656 | tf_op jit(solution)/shard_map/ppermute | solution.py:19
  94.1 36.6 %collective-permute-start.2 = (bf16[128,3072]{1,0:T(8,128)(2,1)S(1)}, bf16[128,3072]{1,0:T(8,128)(2,1)S(1)}, u32[]{:S(2)}, u32[]{:S(2)}) collective-permute-start(bf16[128,3072]{1,0:T(8,128)(2,1)S(1)} %maximum_select_fusion.4), channel_id=1, source_target_pairs={{0,4},{1,5},{2,6},{3,7},{4,0},{5,1},{6,2},{7,3},{8,12},{9,13},{10,... | collective-permute-start | bytes 2359304 | tf_op jit(solution)/shard_map/ppermute | solution.py:19
  141.5 0.7 copy-start.5
  141.5 42.2 %copy-start.3 = (f32[3072]{0:T(1024)S(1)}, f32[3072]{0:T(1024)}, u32[]{:S(2)}) copy-start(f32[3072]{0:T(1024)} %param.12) | copy-start | bytes 36868
  141.5 63.9 %all-gather.5.cloned.1.call-start = ((), (), s32[]{:S(2)}) async-start(), calls=%async_computation.8 | async-start | bytes 1966080 | tf_op jit(solution)/shard_map/all_gather | solution.py:86
  142.8 40.9 %copy-start.1 = (f32[64,3072]{1,0:T(8,128)S(1)}, f32[64,3072]{1,0:T(8,128)}, u32[]{:S(2)}) copy-start(f32[64,3072]{1,0:T(8,128)} %reduce-scatter.9.cloned.1.call-done) | copy-start | bytes 2359300
  183.2 1.1 copy-start.2
  185.6 40.9 %all-gather.3.cloned.1.call-start = ((), (), s32[]{:S(2)}) async-start(), calls=%async_computation.5 | async-start | bytes 1966080 | tf_op jit(solution)/shard_map/all_gather | solution.py:86
  186.2 117.9 %reduce-scatter.11.cloned.1.call-start = ((), (), s32[]{:S(2)}) async-start(), calls=%async_computation.9 | async-start | bytes 3538944 | tf_op jit(solution)/shard_map/reduce_scatter | solution.py:87
  216.0 165.3 %reduce-scatter.7.cloned.1.call-start = ((), (), s32[]{:S(2)}) async-start(), calls=%async_computation.6 | async-start | bytes 3538944 | tf_op jit(solution)/shard_map/reduce_scatter | solution.py:87
  237.1 144.2 %copy-start = (bf16[2,32,3072]{2,1,0:T(8,128)(2,1)S(1)}, bf16[2,32,3072]{2,1,0:T(8,128)(2,1)}, u32[]{:S(2)}) copy-start(bf16[2,32,3072]{2,1,0:T(8,128)(2,1)} %param.8) | copy-start | bytes 1179652
  237.1 144.2 %copy-start.4 = (f32[3072]{0:T(1024)S(1)}, f32[3072]{0:T(1024)}, u32[]{:S(2)}) copy-start(f32[3072]{0:T(1024)} %param.14) | copy-start | bytes 36868
  382.5 0.7 copy-start.6
Sparse Core Ops, SparseCore 0:
  77.8 41.5 reduce-scatter.8
  141.6 41.4 reduce-scatter.4
  185.8 19.6 all-gather.4
  206.8 19.6 all-gather.2
  229.9 74.1 reduce-scatter.10
  307.6 73.6 reduce-scatter.6
